TPU v7x, 32 devices: a whole 2x2x4 slice. The times are simulated.
32 devices in a mesh: slab: 8 (over y, x, core), grp: 4 (over z).
Axes of the slice: x: 2, y: 2, z: 4, core: 2. Of those that a mesh axis runs over, the one named last changes fastest.
Arguments:
- volume: float32 [64, 32, 16, 128], P(None, 'slab', 'grp'), may hold values from -6 to 6
- conv_fine: float32 [3, 3, 3, 64, 64], replicated, may hold values from -0.15625 to 0.15625
- down_first: float32 [2, 2, 2, 64, 128], replicated, may hold values from -0.25 to 0.25
- conv_middle: float32 [3, 3, 3, 128, 128], replicated, may hold values from -0.109375 to 0.109375
- down_second: float32 [2, 2, 2, 128, 256], P(None, None, None, None, 'grp'), may hold values from -0.1875 to 0.1875
- conv_coarse: float32 [3, 3, 3, 256, 512], P(None, None, None, None, 'grp'), may hold values from -0.078125 to 0.078125
Outputs:
- features: float32 [512, 8, 128], P('grp', 'slab')
All inputs are finite; a program needn't handle non-finite values.
Results may differ from a plain program's by a relative error of at most 0.000082.
Values sent between devices are 32-bit elements; how exact they have to be, the bound alone decides.
A program may use at most 64 MiB of HBM per device.

v0:
```python
import functools

import jax
import jax.numpy as jnp
from jax import lax
from jax.experimental import pallas as pl
from jax.experimental.pallas import tpu as pltpu
from jax.sharding import PartitionSpec as P

MESH = pl.DeviceIdType.MESH
F32, BF16 = jnp.float32, jnp.bfloat16
WAYS = ((1, 0), (-1, 0), (0, 1), (0, -1), (1, 1), (1, -1), (-1, 1), (-1, -1))


def split(x):
    high = x.astype(BF16)
    return high, (x - high.astype(F32)).astype(BF16)


def stacked(x):
    return jnp.concatenate(split(x), axis=0)


def product(both, weights, dims=(((1,), (0,)), ((), ()))):
    dot = functools.partial(lax.dot_general, dimension_numbers=dims, preferred_element_type=F32)
    rows = both.shape[0] // 2
    wide = dot(both, weights[0])
    return wide[:rows] + wide[rows:] + dot(both[:rows], weights[1])


def plus(total, term):
    return term if total is None else total + term


def gelu(x):
    return 0.5 * x * (1.0 + lax.erf(x * (0.5**0.5)))


def beside(x, span):
    at = lax.rem(lax.broadcasted_iota(jnp.int32, x.shape, 0), span)
    before = jnp.where(at == 0, 0.0, pltpu.roll(x, 1, 0))
    after = jnp.where(at == span - 1, 0.0, pltpu.roll(x, x.shape[0] - 1, 0))
    return before, after


def kernel(
    slabs, groups,
    vol_hbm, fine_hbm, down1_hbm, middle_hbm, shard, coarse_hbm,
    out,
    vol, fine, field, pair, rows, fine_h, fine_l, down1, down1_h, down1_l, middle, middle_h, middle_l,
    second, rows2, level2, gathered, coarse_w, edges_h, edges_l, centre_h, centre_l,
    coarse, taps, upward, downward, from_lower, from_upper,
    load_sem, send1, recv1, send2, recv2, wsend, wrecv, xsend, xrecv, fsend, frecv, csend, crecv, psend, precv,
):
    s, g = lax.axis_index("slab"), lax.axis_index("grp")
    depth, height, chans, width = (field.shape[0] - 2, field.shape[1] - 2) + field.shape[2:]
    half = width // 2

    loads = [
        pltpu.make_async_copy(vol_hbm, vol, load_sem.at[3]),
        pltpu.make_async_copy(fine_hbm, fine, load_sem.at[4]),
        pltpu.make_async_copy(shard, gathered.at[g], load_sem.at[5]),
        pltpu.make_async_copy(down1_hbm, down1, load_sem.at[0]),
        pltpu.make_async_copy(middle_hbm, middle, load_sem.at[1]),
        pltpu.make_async_copy(coarse_hbm, coarse_w, load_sem.at[2]),
    ]
    for load in loads:
        load.start()

    def exists(ds, dg):
        return (s + ds >= 0) & (s + ds < slabs) & (g + dg >= 0) & (g + dg < groups)

    barrier = pltpu.get_barrier_semaphore()
    heard = jnp.int32(0)
    for ds, dg in WAYS:
        there = exists(ds, dg)
        heard = heard + there.astype(jnp.int32)

        @pl.when(there)
        def _():
            pl.semaphore_signal(barrier, inc=1, device_id=(s + ds, g + dg), device_id_type=MESH)

    for dg in range(2, groups):
        for sign in (1, -1):
            there = exists(0, sign * dg)
            heard = heard + there.astype(jnp.int32)

            @pl.when(there)
            def _():
                pl.semaphore_signal(barrier, inc=1, device_id=(s, g + sign * dg), device_id_type=MESH)

    sibling = s + 1 - 2 * lax.rem(s, 2)
    place = lax.rem(s // 2, 2)
    crossings = [s + 2 - 4 * place]
    for peer in crossings:
        pl.semaphore_signal(barrier, inc=1, device_id=(peer, g), device_id_type=MESH)
    loads[0].wait()
    lines = depth * height
    for r in range(lines):
        field[1 + r // height, 1 + r % height] = vol[pl.ds(r, chans, stride=lines), :]
    pl.semaphore_wait(barrier, heard + len(crossings))

    def part(way, size, offset):
        if way == 0:
            return pl.ds(offset, size)
        return pl.ds(offset + (size - 1 if way > 0 else 0), 1)

    def landing(way, size):
        if way == 0:
            return pl.ds(1, size)
        return pl.ds(0 if way > 0 else size + 1, 1)

    def halo(src, offset, buf, sends, recvs):
        nd, nh = buf.shape[0] - 2, buf.shape[1] - 2
        copies = []
        for k, (ds, dg) in enumerate(WAYS):
            copies.append(
                pltpu.make_async_remote_copy(
                    src_ref=src.at[part(ds, nd, offset), part(dg, nh, offset)],
                    dst_ref=buf.at[landing(ds, nd), landing(dg, nh)],
                    send_sem=sends.at[k],
                    recv_sem=recvs.at[k],
                    device_id=(s + ds, g + dg),
                    device_id_type=MESH,
                )
            )

            @pl.when(exists(ds, dg))
            def _():
                copies[k].start()

            @pl.when(jnp.logical_not(exists(-ds, -dg)))
            def _():
                piece = (landing(ds, nd), landing(dg, nh))
                shape = (piece[0].size, piece[1].size) + buf.shape[2:]
                buf[piece[0], piece[1]] = jnp.zeros(shape, F32)

        return copies

    def arrive(copies, received, ways=range(len(WAYS))):
        for k in ways:
            ds, dg = WAYS[k]
            if received:
                @pl.when(exists(-ds, -dg))
                def _():
                    copies[k].wait_recv()
            else:
                @pl.when(exists(ds, dg))
                def _():
                    copies[k].wait_send()

    first = halo(field, 1, field, send1, recv1)

    taps_of = shard.shape[0]
    parity = lax.rem(s, 2)
    fourth = pl.ds((parity * 2 + place) * (taps_of // 4), taps_of // 4)
    half_taps = pl.ds(parity * (taps_of // 2), taps_of // 2)
    spread, crossed, forward = [], [], []
    for j in range(1, groups):
        copy = pltpu.make_async_remote_copy(
            src_ref=shard.at[fourth],
            dst_ref=gathered.at[g, fourth],
            send_sem=wsend.at[j],
            recv_sem=wrecv.at[j],
            device_id=(s, lax.rem(g + j, groups)),
            device_id_type=MESH,
        )
        copy.start()
        spread.append(copy)

    def hand_on(arrived, out_copies, piece, sends, recvs, peers):
        for j in range(1, groups):
            for copy in arrived[j - 1]:
                copy.wait_recv()
            source = lax.rem(g + groups - j, groups)
            made = []
            for k, peer in enumerate(peers):
                copy = pltpu.make_async_remote_copy(
                    src_ref=gathered.at[source, piece],
                    dst_ref=gathered.at[source, piece],
                    send_sem=sends.at[j, k],
                    recv_sem=recvs.at[j, k],
                    device_id=(peer, g),
                    device_id_type=MESH,
                )
                copy.start()
                made.append(copy)
            out_copies.append(made)

    loads[1].wait()
    blank = jnp.zeros((chans, 2 * chans), BF16)
    nothing = jnp.zeros((chans, chans), F32)
    for a in range(3):
        for b in range(3):
            for pos in range(4):
                left = fine[(a * 3 + b) * 3 + pos] if pos < 3 else nothing
                right = fine[(a * 3 + b) * 3 + pos - 1] if pos > 0 else nothing
                high, low = split(jnp.concatenate([left, right], axis=1))
                for hb in range(2):
                    p, sub = divmod(b + hb, 2)
                    spot = pl.ds((pos * 2 + sub) * chans, chans)
                    fine_h[a, p, spot, hb * 2 * chans : (hb + 1) * 2 * chans] = high
                    fine_l[a, p, spot, hb * 2 * chans : (hb + 1) * 2 * chans] = low
        for pos in range(4):
            for p, sub, hb in ((0, 0, 1), (1, 1, 0)):
                spot = pl.ds((pos * 2 + sub) * chans, chans)
                fine_h[a, p, spot, hb * 2 * chans : (hb + 1) * 2 * chans] = blank
                fine_l[a, p, spot, hb * 2 * chans : (hb + 1) * 2 * chans] = blank

    pairs = height // 2 + 1
    blocks = height // 2
    d2, h2, c2 = depth // 2, blocks, down1.shape[2]
    for load in loads[2:]:
        load.wait()
    for a in range(2):
        down1_h[a], down1_l[a] = split(down1[a])

    @pl.loop(0, 3)
    def _(a):
        for b in range(3):
            high, low = split(middle[a * 3 + b])
            for hb in range(2):
                spot = pl.ds((b + hb) * 3 * c2, 3 * c2)
                middle_h[a, spot, hb * c2 : (hb + 1) * c2] = high
                middle_l[a, spot, hb * c2 : (hb + 1) * c2] = low

    outs = coarse_w.shape[2]

    @pl.loop(0, 3)
    def _(b):
        for a, k in ((0, 0), (2, 1)):
            high, low = split(coarse_w[a * 3 + b])
            edges_h[b, :, k * outs : (k + 1) * outs] = high
            edges_l[b, :, k * outs : (k + 1) * outs] = low
        centre_h[b], centre_l[b] = split(coarse_w[3 + b])

    def build(p):
        @pl.loop(0, depth + 2)
        def _(d):
            pair[p] = field[d, 2 * p : 2 * p + 2].reshape(2 * chans, width).T
            even = pair[p, pl.ds(0, half, stride=2), :]
            odd = pair[p, pl.ds(1, half, stride=2), :]
            before, _ = beside(odd, half)
            _, after = beside(even, half)
            rows[0, d, p], rows[1, d, p] = split(jnp.concatenate([before, even, odd, after], axis=1))

    totals = [None] * blocks

    def convolve(p):
        for a in range(3):
            lhs = rows[:, a : a + depth, p].reshape(2 * depth * half, 8 * chans)
            for block in range(blocks):
                if 0 <= p - block <= 1:
                    w = (fine_h[a, p - block], fine_l[a, p - block])
                    totals[block] = plus(totals[block], product(lhs, w))

    arrive(first, True, range(0, 2))
    for p in range(1, blocks):
        build(p)
        convolve(p)
    arrive(first, True, range(2, len(WAYS)))
    for p in (0, blocks):
        build(p)
        convolve(p)
    ones = [gelu(t).reshape(d2, 2, half, 4 * chans) for t in totals]
    total = None
    for a in range(2):
        lhs = jnp.concatenate([o[:, a].reshape(d2 * half, 4 * chans) for o in ones], axis=0)
        total = plus(total, product(stacked(lhs), (down1_h[a], down1_l[a])))
    total = total.reshape(h2, d2, half, c2)
    for h in range(h2):
        second[1 : d2 + 1, 1 + h] = total[h]
    again = halo(second, 1, second, send2, recv2)
    hand_on([[c] for c in spread], crossed, fourth, xsend, xrecv, crossings)

    def widen(h):
        @pl.loop(0, d2 + 2)
        def _(d):
            x = second[d, h]
            before, after = beside(x, half)
            spot = slice(h * 3 * c2, (h + 1) * 3 * c2)
            rows2[0, d, :, spot], rows2[1, d, :, spot] = split(jnp.concatenate([before, x, after], axis=1))

    def middle_term(a, low, high, left, right):
        lhs = rows2[:, a : a + d2, :, low:high].reshape(2 * d2 * half, high - low)
        return product(lhs, (middle_h[a, low:high, left:right], middle_l[a, low:high, left:right]))

    k3 = 3 * c2
    arrive(again, True, range(0, 2))
    for h in range(1, h2 + 1):
        widen(h)
    total, sides = None, [None, None]
    for a in range(3):
        total = plus(total, middle_term(a, k3, 3 * k3, 0, 2 * c2))
    arrive(again, True, range(2, len(WAYS)))
    for h in (0, h2 + 1):
        widen(h)
    for a in range(3):
        sides[0] = plus(sides[0], middle_term(a, 0, k3, 0, c2))
        sides[1] = plus(sides[1], middle_term(a, 3 * k3, 4 * k3, c2, 2 * c2))
    hand_on(crossed, forward, half_taps, fsend, frecv, [sibling])
    for h in range(h2):
        level2[h] = gelu(total[:, h * c2 : (h + 1) * c2] + sides[h])
    quarter = half // 2
    lhs = jnp.concatenate(
        [
            level2[h, pl.ds(d * half + c, quarter, stride=2), :]
            for d in range(d2) for h in range(h2) for c in range(2)
        ],
        axis=1,
    )
    lhs = stacked(lhs)
    for made in forward:
        made[0].wait_recv()
    weights = jnp.concatenate(
        [gathered[:, t].reshape(groups * shard.shape[1], c2) for t in range(taps_of)], axis=1
    )
    share = product(lhs, split(weights), (((1,), (1,)), ((), ())))
    coarse[pl.ds(g, 1)] = share[None]
    sent = []
    for j in range(1, groups):
        copy = pltpu.make_async_remote_copy(
            src_ref=coarse.at[g],
            dst_ref=coarse.at[g],
            send_sem=csend.at[j],
            recv_sem=crecv.at[j],
            device_id=(s, lax.rem(g + j, groups)),
            device_id_type=MESH,
        )
        copy.start()
        sent.append(copy)
    cells = groups * quarter
    edge = jnp.zeros((2, quarter, taps.shape[2]), BF16)
    taps[:, 0:quarter] = edge
    taps[:, quarter + cells : 2 * quarter + cells] = edge
    for copy in sent:
        copy.wait_recv()
    x = coarse[...].reshape(cells, coarse.shape[2])
    before, after = beside(x, quarter)
    taps[0, quarter : quarter + cells], taps[1, quarter : quarter + cells] = split(
        jnp.concatenate([before, x, after], axis=1)
    )

    def plane(high, low):
        total = None
        for b in range(3):
            lhs = taps[:, b * quarter : b * quarter + cells].reshape(2 * cells, taps.shape[2])
            total = plus(total, product(lhs, (high[b], low[b])))
        return total

    both = plane(edges_h, edges_l)
    upward[...] = both[:, :outs]
    downward[...] = both[:, outs:]
    up = pltpu.make_async_remote_copy(
        src_ref=upward, dst_ref=from_lower, send_sem=psend.at[0], recv_sem=precv.at[0],
        device_id=(s + 1, g), device_id_type=MESH,
    )
    down = pltpu.make_async_remote_copy(
        src_ref=downward, dst_ref=from_upper, send_sem=psend.at[1], recv_sem=precv.at[1],
        device_id=(s - 1, g), device_id_type=MESH,
    )

    @pl.when(exists(1, 0))
    def _():
        up.start()

    @pl.when(jnp.logical_not(exists(-1, 0)))
    def _():
        from_lower[...] = jnp.zeros(from_lower.shape, F32)

    @pl.when(exists(-1, 0))
    def _():
        down.start()

    @pl.when(jnp.logical_not(exists(1, 0)))
    def _():
        from_upper[...] = jnp.zeros(from_upper.shape, F32)

    centre = plane(centre_h, centre_l)

    @pl.when(exists(-1, 0))
    def _():
        up.wait_recv()

    @pl.when(exists(1, 0))
    def _():
        down.wait_recv()

    out[...] = gelu(centre + from_lower[...] + from_upper[...]).T

    arrive(first, False)
    arrive(again, False)
    for copy in spread + sum(crossed + forward, []) + sent:
        copy.wait_send()

    @pl.when(exists(1, 0))
    def _():
        up.wait_send()

    @pl.when(exists(-1, 0))
    def _():
        down.wait_send()


def per_device(slabs, groups, volume, conv_fine, down_first, conv_middle, down_second, conv_coarse):
    c1, depth, height, width = volume.shape
    c2, c3, c4 = down_first.shape[4], conv_coarse.shape[3], conv_coarse.shape[4]
    half, quarter = width // 2, width // 4
    d2, h2 = depth // 2, height // 2
    part = down_second.shape[4]
    cells = groups * quarter
    vol = volume.reshape(c1 * depth * height, width)
    fine = conv_fine.reshape(27, c1, c1)
    down1 = down_first.reshape(2, 4 * c1, c2)
    middle = conv_middle.reshape(9, 3 * c2, c2)
    shard = jnp.swapaxes(down_second, 3, 4).reshape(8, part, c2)
    pairs = h2 + 1
    coarse_w = conv_coarse.reshape(9, 3 * c3, c4)
    V = pltpu.VMEM
    vmem, away = pl.BlockSpec(memory_space=pltpu.VMEM), pl.BlockSpec(memory_space=pl.ANY)
    dma = pltpu.SemaphoreType.DMA
    result = pl.pallas_call(
        functools.partial(kernel, slabs, groups),
        out_shape=jax.ShapeDtypeStruct((c4, cells), F32),
        in_specs=[away] * 6,
        out_specs=vmem,
        scratch_shapes=[
            V(vol.shape, F32),
            V(fine.shape, F32),
            V((depth + 2, height + 2, c1, width), F32),
            V((pairs, width, 2 * c1), F32),
            V((2, depth + 2, pairs, half, 8 * c1), BF16),
            V((3, 2, 8 * c1, 4 * c1), BF16),
            V((3, 2, 8 * c1, 4 * c1), BF16),
            V(down1.shape, F32),
            V(down1.shape, BF16),
            V(down1.shape, BF16),
            V(middle.shape, F32),
            V((3, 12 * c2, 2 * c2), BF16),
            V((3, 12 * c2, 2 * c2), BF16),
            V((d2 + 2, h2 + 2, half, c2), F32),
            V((2, d2 + 2, half, 12 * c2), BF16),
            V((h2, d2 * half, c2), F32),
            V((groups,) + shard.shape, F32),
            V(coarse_w.shape, F32),
            V((3, 3 * c3, 2 * c4), BF16),
            V((3, 3 * c3, 2 * c4), BF16),
            V((3, 3 * c3, c4), BF16),
            V((3, 3 * c3, c4), BF16),
            V((groups, quarter, c3), F32),
            V((2, cells + 2 * quarter, 3 * c3), BF16),
            V((cells, c4), F32),
            V((cells, c4), F32),
            V((cells, c4), F32),
            V((cells, c4), F32),
            dma((6,)),
            dma((8,)), dma((8,)), dma((8,)), dma((8,)),
            dma((groups,)), dma((groups,)), dma((groups, 3)), dma((groups, 3)), dma((groups, 1)), dma((groups, 1)), dma((groups,)), dma((groups,)),
            dma((2,)), dma((2,)),
        ],
        compiler_params=pltpu.CompilerParams(
            collective_id=0, has_side_effects=True, vmem_limit_bytes=60 * 1024 * 1024
        ),
    )(vol, fine, down1, middle, shard, coarse_w)
    return result.reshape(c4, 1, cells)


def solution(mesh):
    placed = (
        P(None, "slab", "grp", None),
        P(),
        P(),
        P(),
        P(None, None, None, None, "grp"),
        P(None, None, None, None, "grp"),
    )
    body = functools.partial(per_device, mesh.shape["slab"], mesh.shape["grp"])
    return jax.shard_map(
        body, mesh=mesh, in_specs=placed, out_specs=P("grp", "slab", None), check_vma=False
    )
```

profile of v0, /device:TPU:1, one launch (start us, length us, event | category | flops | bytes accessed | tf_op | source)
XLA Modules:
  0.0 37.6 jit_solution(3728488284318303368)
XLA Ops:
  0.0 36.2 %shard_map.64 = f32[128,128]{1,0:T(8,128)} custom-call(f32[1024,128]{1,0:T(8,128)} %bitcast.14, f32[27,64,64]{2,1,0:T(8,128)} %bitcast.13, f32[2,256,128]{2,1,0:T(8,128)} %bitcast.16, f32[9,384,128]{2,1,0:T(8,128)} %bitcast.12, f32[8,64,128]{2,1,0:T(8,128)} %bitcast.17, f32[9,768,128]{2,1,0:T(8,128)} %bitcast.11), custom_call_target="tpu_custom_call" | custom-call | tf_op jit(solution)/shard_map/pallas_call | solution.py:422
  36.2 1.5 %copy.9 = f32[128,1,128]{2,1,0:T(1,128)} copy(f32[128,1,128]{2,1,0:T(1,128)} %bitcast.15) | data formatting | bytes 131072
where the time goes:
time: 37.8 us; the launch traced here: 37.6 us
  Pallas kernels  36.2 us (96%)
  local copies, waits for them, and re-layouts  1.47 us (4%)
    pallas_call x1, Pallas kernels, per_device(): pl.pallas_call(functools.partial(kernel, slabs, groups), out_shape=jax.Sh...  36.2 us
    unnamed x1, local copies, waits for them, and re-layouts  1.47 us

commit v1 on v0

--- a/solution.py
+++ b/solution.py
@@ -421,7 +421,7 @@
     dma = pltpu.SemaphoreType.DMA
     result = pl.pallas_call(
         functools.partial(kernel, slabs, groups),
-        out_shape=jax.ShapeDtypeStruct((c4, cells), F32),
+        out_shape=pltpu.VMEM((c4, cells), F32),
         in_specs=[away] * 6,
         out_specs=vmem,
         scratch_shapes=[

time: 37.8 us -> 36.3 us (0.960)
  local copies, waits for them, and re-layouts: 1.47 us -> 0.63 us
  Pallas kernels: 36.2 us -> 35.5 us
    unnamed x1, local copies, waits for them, and re-layouts: 1.47 us -> 0.63 us
    pallas_call x1, Pallas kernels: 36.2 us -> 35.5 us  [per_device(): pl.pallas_call(functools.partial(kernel, slabs, groups), out_shape=pltpu....]
where the time goes in v1:
time: 36.3 us; the launch traced here: 36.2 us
  Pallas kernels  35.5 us (98%)
  local copies, waits for them, and re-layouts  0.63 us (2%)
    pallas_call x1, Pallas kernels, per_device(): pl.pallas_call(functools.partial(kernel, slabs, groups), out_shape=pltpu....  35.5 us

profile of v1, /device:TPU:1, one launch (start us, length us, event | category | flops | bytes accessed | tf_op | source)
XLA Modules:
  0.0 36.2 jit_solution(12175562899813982525)
XLA Ops:
  0.0 35.5 %shard_map.64 = f32[128,128]{1,0:T(8,128)S(1)} custom-call(f32[1024,128]{1,0:T(8,128)} %bitcast.15, f32[27,64,64]{2,1,0:T(8,128)} %bitcast.14, f32[2,256,128]{2,1,0:T(8,128)} %bitcast.16, f32[9,384,128]{2,1,0:T(8,128)} %bitcast.13, f32[8,64,128]{2,1,0:T(8,128)} %bitcast.17, f32[9,768,128]{2,1,0:T(8,128)} %bitcast.12), custom_call_target="tpu_custom_call" | custom-call | tf_op jit(solution)/shard_map/pallas_call | solution.py:422
  35.6 0.6 %copy.9 = f32[128,1,128]{2,1,0:T(1,128)} copy(f32[128,1,128]{2,1,0:T(1,128)S(1)} %bitcast.11) | data formatting | bytes 131072

commit v2 on v1

--- a/solution.py
+++ b/solution.py
@@ -36,6 +36,13 @@
     return 0.5 * x * (1.0 + lax.erf(x * (0.5**0.5)))
 
 
+def apart(x, width, chans):
+    lane = lax.broadcasted_iota(jnp.int32, (chans, width), 1)
+    before = jnp.where(lane == 0, 0.0, pltpu.roll(x[:chans], 1, 1))
+    after = jnp.where(lane == width - 1, 0.0, pltpu.roll(x[2 * chans :], width - 1, 1))
+    return before + x[chans : 2 * chans] + after
+
+
 def beside(x, span):
     at = lax.rem(lax.broadcasted_iota(jnp.int32, x.shape, 0), span)
     before = jnp.where(at == 0, 0.0, pltpu.roll(x, 1, 0))
@@ -47,7 +54,7 @@
     slabs, groups,
     vol_hbm, fine_hbm, down1_hbm, middle_hbm, shard, coarse_hbm,
     out,
-    vol, fine, field, pair, rows, fine_h, fine_l, down1, down1_h, down1_l, middle, middle_h, middle_l,
+    vol, fine, field, field_h, field_l, inner, outer, partial, turned, down1, down1_w, middle, middle_h, middle_l,
     second, rows2, level2, gathered, coarse_w, edges_h, edges_l, centre_h, centre_l,
     coarse, taps, upward, downward, from_lower, from_upper,
     load_sem, send1, recv1, send2, recv2, wsend, wrecv, xsend, xrecv, fsend, frecv, csend, crecv, psend, precv,
@@ -90,8 +97,8 @@
                 pl.semaphore_signal(barrier, inc=1, device_id=(s, g + sign * dg), device_id_type=MESH)
 
     sibling = s + 1 - 2 * lax.rem(s, 2)
-    place = lax.rem(s // 2, 2)
-    crossings = [s + 2 - 4 * place]
+    place = lax.rem(s // 4, 2)
+    crossings = [s + 4 - 8 * place]
     for peer in crossings:
         pl.semaphore_signal(barrier, inc=1, device_id=(peer, g), device_id_type=MESH)
     loads[0].wait()
@@ -188,33 +195,40 @@
             out_copies.append(made)
 
     loads[1].wait()
-    blank = jnp.zeros((chans, 2 * chans), BF16)
-    nothing = jnp.zeros((chans, chans), F32)
-    for a in range(3):
-        for b in range(3):
-            for pos in range(4):
-                left = fine[(a * 3 + b) * 3 + pos] if pos < 3 else nothing
-                right = fine[(a * 3 + b) * 3 + pos - 1] if pos > 0 else nothing
-                high, low = split(jnp.concatenate([left, right], axis=1))
-                for hb in range(2):
-                    p, sub = divmod(b + hb, 2)
-                    spot = pl.ds((pos * 2 + sub) * chans, chans)
-                    fine_h[a, p, spot, hb * 2 * chans : (hb + 1) * 2 * chans] = high
-                    fine_l[a, p, spot, hb * 2 * chans : (hb + 1) * 2 * chans] = low
-        for pos in range(4):
-            for p, sub, hb in ((0, 0, 1), (1, 1, 0)):
-                spot = pl.ds((pos * 2 + sub) * chans, chans)
-                fine_h[a, p, spot, hb * 2 * chans : (hb + 1) * 2 * chans] = blank
-                fine_l[a, p, spot, hb * 2 * chans : (hb + 1) * 2 * chans] = blank
-
-    pairs = height // 2 + 1
     blocks = height // 2
+    blank = jnp.zeros((3 * chans, chans), BF16)
+    wide = jnp.concatenate(
+        [
+            jnp.concatenate([fine[ab * 3 + c] for c in range(3)], axis=1)
+            for ab in range(9)
+        ],
+        axis=0,
+    )
+    both = split(wide.T)
+
+    def taps_at(x, b):
+        return [x[:, (a * 3 + b) * chans : (a * 3 + b + 1) * chans] for a in range(3)] if 0 <= b < 3 else [blank] * 3
+
+    within = [[n for n in range(4) if 1 <= 2 * block + n <= height] for block in range(blocks)]
+    beyond = [(0, 0, 0), (3, 1, 2)]
+    for block in range(blocks):
+        for hb in range(2):
+            parts = []
+            for x in both:
+                by_line = [taps_at(x, n - hb) for n in within[block]]
+                parts.append(jnp.concatenate([line[a] for a in range(3) for line in by_line], axis=1))
+            inner[block, hb * 3 * chans : (hb + 1) * 3 * chans] = jnp.concatenate([parts[0], parts[1], parts[0]], axis=1)
+    for k, (_, _, b) in enumerate(beyond):
+        parts = [jnp.concatenate(taps_at(x, b), axis=1) for x in both]
+        outer[k] = jnp.concatenate([parts[0], parts[1], parts[0]], axis=1)
     d2, h2, c2 = depth // 2, blocks, down1.shape[2]
     for load in loads[2:]:
         load.wait()
     for a in range(2):
-        down1_h[a], down1_l[a] = split(down1[a])
-
+        for b in range(2):
+            for c in range(2):
+                spot = pl.ds(((a * 2 + c) * 2 + b) * chans, chans)
+                down1_w[spot, 0:c2], down1_w[spot, c2 : 2 * c2] = split(down1[a, (b * 2 + c) * chans : (b * 2 + c + 1) * chans])
     @pl.loop(0, 3)
     def _(a):
         for b in range(3):
@@ -234,39 +248,50 @@
             edges_l[b, :, k * outs : (k + 1) * outs] = low
         centre_h[b], centre_l[b] = split(coarse_w[3 + b])
 
-    def build(p):
-        @pl.loop(0, depth + 2)
-        def _(d):
-            pair[p] = field[d, 2 * p : 2 * p + 2].reshape(2 * chans, width).T
-            even = pair[p, pl.ds(0, half, stride=2), :]
-            odd = pair[p, pl.ds(1, half, stride=2), :]
-            before, _ = beside(odd, half)
-            _, after = beside(even, half)
-            rows[0, d, p], rows[1, d, p] = split(jnp.concatenate([before, even, odd, after], axis=1))
-
-    totals = [None] * blocks
-
-    def convolve(p):
-        for a in range(3):
-            lhs = rows[:, a : a + depth, p].reshape(2 * depth * half, 8 * chans)
-            for block in range(blocks):
-                if 0 <= p - block <= 1:
-                    w = (fine_h[a, p - block], fine_l[a, p - block])
-                    totals[block] = plus(totals[block], product(lhs, w))
-
+    def narrow(ds, hs):
+        field_h[ds, hs], field_l[ds, hs] = split(field[ds, hs])
+
+    def across(first, count, d):
+        columns = []
+        for e in range(2):
+            place = (slice(d + e, d + e + 3), slice(first, first + count))
+            high = field_h[place].reshape(3 * count * chans, width)
+            low = field_l[place].reshape(3 * count * chans, width)
+            columns.append(jnp.concatenate([high, high, low], axis=0))
+        return jnp.concatenate(columns, axis=1)
+
+    dot = functools.partial(jnp.dot, preferred_element_type=F32)
+    narrow(slice(1, depth + 1), slice(1, height + 1))
     arrive(first, True, range(0, 2))
-    for p in range(1, blocks):
-        build(p)
-        convolve(p)
+    for d in (0, depth + 1):
+        narrow(slice(d, d + 1), slice(1, height + 1))
+    for block in range(blocks):
+        for k in range(d2):
+            partial[block, k] = dot(inner[block], across(2 * block + within[block][0], len(within[block]), 2 * k))
     arrive(first, True, range(2, len(WAYS)))
-    for p in (0, blocks):
-        build(p)
-        convolve(p)
-    ones = [gelu(t).reshape(d2, 2, half, 4 * chans) for t in totals]
-    total = None
-    for a in range(2):
-        lhs = jnp.concatenate([o[:, a].reshape(d2 * half, 4 * chans) for o in ones], axis=0)
-        total = plus(total, product(stacked(lhs), (down1_h[a], down1_l[a])))
+    for h in (0, height + 1):
+        narrow(slice(0, depth + 2), slice(h, h + 1))
+    halves = []
+    for block in range(blocks):
+        n, extra_hb, _ = beyond[block]
+        for k in range(d2):
+            extra = dot(outer[block], across(2 * block + n, 1, 2 * k))
+            row = []
+            for e in range(2):
+                ends = []
+                for hb in range(2):
+                    x = partial[block, k, hb * 3 * chans : (hb + 1) * 3 * chans, e * width : (e + 1) * width]
+                    if hb == extra_hb:
+                        x = x + extra[:, e * width : (e + 1) * width]
+                    ends.append(apart(x, width, chans))
+                spot = (block * d2 + k) * 2 + e
+                turned[spot] = gelu(jnp.concatenate(ends, axis=0)).T
+                row += [turned[spot, pl.ds(c, half, stride=2), :] for c in range(2)]
+            halves.append(jnp.concatenate(row, axis=1))
+    lhs = jnp.concatenate(halves, axis=0)
+    wide = dot(stacked(lhs), down1_w[...])
+    cells1 = lhs.shape[0]
+    total = wide[:cells1, :c2] + wide[:cells1, c2:] + wide[cells1:, :c2]
     total = total.reshape(h2, d2, half, c2)
     for h in range(h2):
         second[1 : d2 + 1, 1 + h] = total[h]
@@ -414,7 +439,6 @@
     down1 = down_first.reshape(2, 4 * c1, c2)
     middle = conv_middle.reshape(9, 3 * c2, c2)
     shard = jnp.swapaxes(down_second, 3, 4).reshape(8, part, c2)
-    pairs = h2 + 1
     coarse_w = conv_coarse.reshape(9, 3 * c3, c4)
     V = pltpu.VMEM
     vmem, away = pl.BlockSpec(memory_space=pltpu.VMEM), pl.BlockSpec(memory_space=pl.ANY)
@@ -428,13 +452,14 @@
             V(vol.shape, F32),
             V(fine.shape, F32),
             V((depth + 2, height + 2, c1, width), F32),
-            V((pairs, width, 2 * c1), F32),
-            V((2, depth + 2, pairs, half, 8 * c1), BF16),
-            V((3, 2, 8 * c1, 4 * c1), BF16),
-            V((3, 2, 8 * c1, 4 * c1), BF16),
+            V((depth + 2, height + 2, c1, width), BF16),
+            V((depth + 2, height + 2, c1, width), BF16),
+            V((2, 6 * c1, 27 * c1), BF16),
+            V((2, 3 * c1, 9 * c1), BF16),
+            V((2, d2, 6 * c1, 2 * width), F32),
+            V((2 * d2 * 2, width, 2 * c1), F32),
             V(down1.shape, F32),
-            V(down1.shape, BF16),
-            V(down1.shape, BF16),
+            V((8 * c1, 2 * c2), BF16),
             V(middle.shape, F32),
             V((3, 12 * c2, 2 * c2), BF16),
             V((3, 12 * c2, 2 * c2), BF16),

time: 36.3 us -> 33.2 us (0.915)
  Pallas kernels: 35.5 us -> 32.5 us
    pallas_call x1, Pallas kernels: 35.5 us -> 32.5 us  [per_device(): pl.pallas_call(functools.partial(kernel, slabs, groups), out_shape=pltpu....]
where the time goes in v2:
time: 33.2 us; the launch traced here: 33.1 us
  Pallas kernels  32.5 us (98%)
  local copies, waits for them, and re-layouts  0.63 us (2%)
    pallas_call x1, Pallas kernels, per_device(): pl.pallas_call(functools.partial(kernel, slabs, groups), out_shape=pltpu....  32.5 us

profile of v2, /device:TPU:1, one launch (start us, length us, event | category | flops | bytes accessed | tf_op | source)
XLA Modules:
  0.0 33.1 jit_solution(4439208412176663311)
XLA Ops:
  0.0 32.5 %shard_map.64 = f32[128,128]{1,0:T(8,128)S(1)} custom-call(f32[1024,128]{1,0:T(8,128)} %bitcast.15, f32[27,64,64]{2,1,0:T(8,128)} %bitcast.14, f32[2,256,128]{2,1,0:T(8,128)} %bitcast.16, f32[9,384,128]{2,1,0:T(8,128)} %bitcast.13, f32[8,64,128]{2,1,0:T(8,128)} %bitcast.17, f32[9,768,128]{2,1,0:T(8,128)} %bitcast.12), custom_call_target="tpu_custom_call" | custom-call | tf_op jit(solution)/shard_map/pallas_call | solution.py:446
  32.5 0.6 %copy.9 = f32[128,1,128]{2,1,0:T(1,128)} copy(f32[128,1,128]{2,1,0:T(1,128)S(1)} %bitcast.11) | data formatting | bytes 131072

commit v3 on v2

--- a/solution.py
+++ b/solution.py
@@ -54,10 +54,10 @@
     slabs, groups,
     vol_hbm, fine_hbm, down1_hbm, middle_hbm, shard, coarse_hbm,
     out,
-    vol, fine, field, field_h, field_l, inner, outer, partial, turned, down1, down1_w, middle, middle_h, middle_l,
-    second, rows2, level2, gathered, coarse_w, edges_h, edges_l, centre_h, centre_l,
-    coarse, taps, upward, downward, from_lower, from_upper,
-    load_sem, send1, recv1, send2, recv2, wsend, wrecv, xsend, xrecv, fsend, frecv, csend, crecv, psend, precv,
+    vol, fine, field, field_h, field_l, inner, outer, partial, turned, down1, down1_w, middle,
+    mid_h, mid_l, side_h, side_l, second, second_h, second_l, level2, gathered, coarse_w, coarse_b,
+    coarse, sums,
+    load_sem, send1, recv1, send2, recv2, wsend, wrecv, xsend, xrecv, fsend, frecv, csend, crecv, nsend, nrecv,
 ):
     s, g = lax.axis_index("slab"), lax.axis_index("grp")
     depth, height, chans, width = (field.shape[0] - 2, field.shape[1] - 2) + field.shape[2:]
@@ -97,16 +97,33 @@
                 pl.semaphore_signal(barrier, inc=1, device_id=(s, g + sign * dg), device_id_type=MESH)
 
     sibling = s + 1 - 2 * lax.rem(s, 2)
-    place = lax.rem(s // 4, 2)
-    crossings = [s + 4 - 8 * place]
+    low, high = lax.rem(s // 2, 2), lax.rem(s // 4, 2)
+    crossings = [s + 2 - 4 * low, s + 4 - 8 * high, s + 6 - 4 * low - 8 * high]
     for peer in crossings:
         pl.semaphore_signal(barrier, inc=1, device_id=(peer, g), device_id_type=MESH)
+    pl.semaphore_wait(barrier, heard + len(crossings))
+
+    taps_of = shard.shape[0]
+    parity = lax.rem(s, 2)
+    eighth = pl.ds((parity * 4 + lax.rem(s // 2, 4)) * (taps_of // 8), taps_of // 8)
+    half_taps = pl.ds(parity * (taps_of // 2), taps_of // 2)
+    spread, crossed, forward = [], [], []
+    for j in range(1, groups):
+        copy = pltpu.make_async_remote_copy(
+            src_ref=shard.at[eighth],
+            dst_ref=gathered.at[g, eighth],
+            send_sem=wsend.at[j],
+            recv_sem=wrecv.at[j],
+            device_id=(s, lax.rem(g + j, groups)),
+            device_id_type=MESH,
+        )
+        copy.start()
+        spread.append(copy)
+
     loads[0].wait()
     lines = depth * height
     for r in range(lines):
         field[1 + r // height, 1 + r % height] = vol[pl.ds(r, chans, stride=lines), :]
-    pl.semaphore_wait(barrier, heard + len(crossings))
-
     def part(way, size, offset):
         if way == 0:
             return pl.ds(offset, size)
@@ -157,23 +174,6 @@
                     copies[k].wait_send()
 
     first = halo(field, 1, field, send1, recv1)
-
-    taps_of = shard.shape[0]
-    parity = lax.rem(s, 2)
-    fourth = pl.ds((parity * 2 + place) * (taps_of // 4), taps_of // 4)
-    half_taps = pl.ds(parity * (taps_of // 2), taps_of // 2)
-    spread, crossed, forward = [], [], []
-    for j in range(1, groups):
-        copy = pltpu.make_async_remote_copy(
-            src_ref=shard.at[fourth],
-            dst_ref=gathered.at[g, fourth],
-            send_sem=wsend.at[j],
-            recv_sem=wrecv.at[j],
-            device_id=(s, lax.rem(g + j, groups)),
-            device_id_type=MESH,
-        )
-        copy.start()
-        spread.append(copy)
 
     def hand_on(arrived, out_copies, piece, sends, recvs, peers):
         for j in range(1, groups):
@@ -222,31 +222,45 @@
         parts = [jnp.concatenate(taps_at(x, b), axis=1) for x in both]
         outer[k] = jnp.concatenate([parts[0], parts[1], parts[0]], axis=1)
     d2, h2, c2 = depth // 2, blocks, down1.shape[2]
-    for load in loads[2:]:
+    for load in loads[2:5]:
         load.wait()
     for a in range(2):
         for b in range(2):
             for c in range(2):
                 spot = pl.ds(((a * 2 + c) * 2 + b) * chans, chans)
                 down1_w[spot, 0:c2], down1_w[spot, c2 : 2 * c2] = split(down1[a, (b * 2 + c) * chans : (b * 2 + c + 1) * chans])
+
     @pl.loop(0, 3)
     def _(a):
-        for b in range(3):
-            high, low = split(middle[a * 3 + b])
-            for hb in range(2):
-                spot = pl.ds((b + hb) * 3 * c2, 3 * c2)
-                middle_h[a, spot, hb * c2 : (hb + 1) * c2] = high
-                middle_l[a, spot, hb * c2 : (hb + 1) * c2] = low
+        for line in range(1, h2 + 1):
+            rows = pl.ds(pl.multiple_of((a * h2 + line - 1) * c2, c2), c2)
+            for hb in range(h2):
+                for c in range(3):
+                    columns = pl.ds((hb * 3 + c) * c2, c2)
+                    if 0 <= line - hb < 3:
+                        mid_h[rows, columns], mid_l[rows, columns] = split(middle[a * 3 + line - hb, c * c2 : (c + 1) * c2])
+                    else:
+                        mid_h[rows, columns] = mid_l[rows, columns] = jnp.zeros((c2, c2), BF16)
+        rows = pl.ds(pl.multiple_of(a * c2, c2), c2)
+        for k, b in ((0, 0), (1, 2)):
+            for c in range(3):
+                columns = pl.ds(c * c2, c2)
+                side_h[k, rows, columns], side_l[k, rows, columns] = split(middle[a * 3 + b, c * c2 : (c + 1) * c2])
 
     outs = coarse_w.shape[2]
-
-    @pl.loop(0, 3)
-    def _(b):
-        for a, k in ((0, 0), (2, 1)):
-            high, low = split(coarse_w[a * 3 + b])
-            edges_h[b, :, k * outs : (k + 1) * outs] = high
-            edges_l[b, :, k * outs : (k + 1) * outs] = low
-        centre_h[b], centre_l[b] = split(coarse_w[3 + b])
+    c3 = coarse.shape[3]
+
+    def prepare_coarse():
+        loads[5].wait()
+
+        @pl.loop(0, 3)
+        def _(a):
+            for b in range(3):
+                for c in range(3):
+                    high, low = split(coarse_w[a * 3 + b, c * c3 : (c + 1) * c3])
+                    spot = (b * 3 + c) * outs
+                    coarse_b[a, :, spot : spot + outs] = high
+                    coarse_b[a, :, 9 * outs + spot : 10 * outs + spot] = low
 
     def narrow(ds, hs):
         field_h[ds, hs], field_l[ds, hs] = split(field[ds, hs])
@@ -254,7 +268,7 @@
     def across(first, count, d):
         columns = []
         for e in range(2):
-            place = (slice(d + e, d + e + 3), slice(first, first + count))
+            place = (pl.ds(d + e, 3), slice(first, first + count))
             high = field_h[place].reshape(3 * count * chans, width)
             low = field_l[place].reshape(3 * count * chans, width)
             columns.append(jnp.concatenate([high, high, low], axis=0))
@@ -262,12 +276,20 @@
 
     dot = functools.partial(jnp.dot, preferred_element_type=F32)
     narrow(slice(1, depth + 1), slice(1, height + 1))
-    arrive(first, True, range(0, 2))
-    for d in (0, depth + 1):
-        narrow(slice(d, d + 1), slice(1, height + 1))
-    for block in range(blocks):
-        for k in range(d2):
+    pairs = [jnp.where(parity == 0, d2 - 1, 0)] + list(range(1, d2 - 1))
+    pairs.append(d2 - 1 - pairs[0])
+    for n, k in enumerate(pairs):
+        if n in (0, d2 - 1):
+            for way in range(2):
+                mine = (parity == 1 - way) if n == 0 else (parity == way)
+
+                @pl.when(mine)
+                def _():
+                    arrive(first, True, (way,))
+            narrow(pl.ds(jnp.where(k == 0, 0, depth + 1), 1), slice(1, height + 1))
+        for block in range(blocks):
             partial[block, k] = dot(inner[block], across(2 * block + within[block][0], len(within[block]), 2 * k))
+    hand_on([[c] for c in spread], crossed, eighth, xsend, xrecv, crossings)
     arrive(first, True, range(2, len(WAYS)))
     for h in (0, height + 1):
         narrow(slice(0, depth + 2), slice(h, h + 1))
@@ -296,36 +318,39 @@
     for h in range(h2):
         second[1 : d2 + 1, 1 + h] = total[h]
     again = halo(second, 1, second, send2, recv2)
-    hand_on([[c] for c in spread], crossed, fourth, xsend, xrecv, crossings)
-
-    def widen(h):
-        @pl.loop(0, d2 + 2)
-        def _(d):
-            x = second[d, h]
-            before, after = beside(x, half)
-            spot = slice(h * 3 * c2, (h + 1) * 3 * c2)
-            rows2[0, d, :, spot], rows2[1, d, :, spot] = split(jnp.concatenate([before, x, after], axis=1))
-
-    def middle_term(a, low, high, left, right):
-        lhs = rows2[:, a : a + d2, :, low:high].reshape(2 * d2 * half, high - low)
-        return product(lhs, (middle_h[a, low:high, left:right], middle_l[a, low:high, left:right]))
-
-    k3 = 3 * c2
+    prepare_coarse()
+    def thin(h):
+        spot = slice(h * c2, (h + 1) * c2)
+        second_h[:, :, spot], second_l[:, :, spot] = split(second[:, h])
+
+    def gathered_taps(low, high):
+        parts = []
+        for x in (second_h, second_l):
+            parts.append(
+                jnp.concatenate([x[a : a + d2, :, low:high].reshape(d2 * half, high - low) for a in range(3)], axis=1)
+            )
+        return jnp.concatenate(parts, axis=0)
+
     arrive(again, True, range(0, 2))
     for h in range(1, h2 + 1):
-        widen(h)
-    total, sides = None, [None, None]
-    for a in range(3):
-        total = plus(total, middle_term(a, k3, 3 * k3, 0, 2 * c2))
+        thin(h)
+    total = product(gathered_taps(c2, (1 + h2) * c2), (mid_h[...], mid_l[...]))
+    hand_on(crossed, forward, half_taps, fsend, frecv, [sibling])
     arrive(again, True, range(2, len(WAYS)))
     for h in (0, h2 + 1):
-        widen(h)
-    for a in range(3):
-        sides[0] = plus(sides[0], middle_term(a, 0, k3, 0, c2))
-        sides[1] = plus(sides[1], middle_term(a, 3 * k3, 4 * k3, c2, 2 * c2))
-    hand_on(crossed, forward, half_taps, fsend, frecv, [sibling])
+        thin(h)
+    sides = [
+        product(gathered_taps(h * c2, (h + 1) * c2), (side_h[k], side_l[k])) for k, h in ((0, 0), (1, h2 + 1))
+    ]
     for h in range(h2):
-        level2[h] = gelu(total[:, h * c2 : (h + 1) * c2] + sides[h])
+        x = total[:, h * 3 * c2 : (h + 1) * 3 * c2]
+        if h == 0:
+            x = x + sides[0]
+        if h == h2 - 1:
+            x = x + sides[1]
+        before, _ = beside(x[:, :c2], half)
+        _, after = beside(x[:, 2 * c2 :], half)
+        level2[h] = gelu(before + x[:, c2 : 2 * c2] + after)
     quarter = half // 2
     lhs = jnp.concatenate(
         [
@@ -341,90 +366,104 @@
         [gathered[:, t].reshape(groups * shard.shape[1], c2) for t in range(taps_of)], axis=1
     )
     share = product(lhs, split(weights), (((1,), (1,)), ((), ())))
-    coarse[pl.ds(g, 1)] = share[None]
+    coarse[1, pl.ds(g, 1)] = share[None]
+    cells = groups * quarter
+
+    def nth(n):
+        spare = jnp.minimum(g, groups - 1 - g)
+        near = (n + 1) // 2 if n % 2 else -(n // 2)
+        away = jnp.where(2 * g < groups - 1, 1, -1)
+        return g + jnp.where(n <= 2 * spare, near, away * (n - spare))
+
     sent = []
-    for j in range(1, groups):
+
+    def send(there, line, plane, peer, sends, recvs):
         copy = pltpu.make_async_remote_copy(
-            src_ref=coarse.at[g],
-            dst_ref=coarse.at[g],
-            send_sem=csend.at[j],
-            recv_sem=crecv.at[j],
-            device_id=(s, lax.rem(g + j, groups)),
-            device_id_type=MESH,
+            src_ref=coarse.at[1, line], dst_ref=coarse.at[plane, line], send_sem=sends, recv_sem=recvs,
+            device_id=peer, device_id_type=MESH,
         )
-        copy.start()
-        sent.append(copy)
-    cells = groups * quarter
-    edge = jnp.zeros((2, quarter, taps.shape[2]), BF16)
-    taps[:, 0:quarter] = edge
-    taps[:, quarter + cells : 2 * quarter + cells] = edge
-    for copy in sent:
-        copy.wait_recv()
-    x = coarse[...].reshape(cells, coarse.shape[2])
-    before, after = beside(x, quarter)
-    taps[0, quarter : quarter + cells], taps[1, quarter : quarter + cells] = split(
-        jnp.concatenate([before, x, after], axis=1)
-    )
-
-    def plane(high, low):
-        total = None
-        for b in range(3):
-            lhs = taps[:, b * quarter : b * quarter + cells].reshape(2 * cells, taps.shape[2])
-            total = plus(total, product(lhs, (high[b], low[b])))
-        return total
-
-    both = plane(edges_h, edges_l)
-    upward[...] = both[:, :outs]
-    downward[...] = both[:, outs:]
-    up = pltpu.make_async_remote_copy(
-        src_ref=upward, dst_ref=from_lower, send_sem=psend.at[0], recv_sem=precv.at[0],
-        device_id=(s + 1, g), device_id_type=MESH,
-    )
-    down = pltpu.make_async_remote_copy(
-        src_ref=downward, dst_ref=from_upper, send_sem=psend.at[1], recv_sem=precv.at[1],
-        device_id=(s - 1, g), device_id_type=MESH,
-    )
-
-    @pl.when(exists(1, 0))
-    def _():
-        up.start()
-
-    @pl.when(jnp.logical_not(exists(-1, 0)))
-    def _():
-        from_lower[...] = jnp.zeros(from_lower.shape, F32)
-
-    @pl.when(exists(-1, 0))
-    def _():
-        down.start()
-
-    @pl.when(jnp.logical_not(exists(1, 0)))
-    def _():
-        from_upper[...] = jnp.zeros(from_upper.shape, F32)
-
-    centre = plane(centre_h, centre_l)
-
-    @pl.when(exists(-1, 0))
-    def _():
-        up.wait_recv()
-
-    @pl.when(exists(1, 0))
-    def _():
-        down.wait_recv()
-
-    out[...] = gelu(centre + from_lower[...] + from_upper[...]).T
+
+        @pl.when(there)
+        def _():
+            copy.start()
+
+        sent.append((there, copy))
+
+    order = [nth(n) for n in range(groups)]
+
+    def sideways(n):
+        for k, ds in enumerate((1, -1)):
+            send(exists(ds, 0), order[n], 1 - ds, (s + ds, g), nsend.at[k, n], nrecv.at[1 - ds, order[n]])
+
+    for k, dg in enumerate(d for d in range(1 - groups, groups) if d):
+        send(exists(0, dg), g, 1, (s, g + dg), csend.at[k], crecv.at[g])
+    sideways(0)
+
+    def landed(n, plane):
+        line = order[n]
+        sems = crecv.at[line] if plane == 1 else nrecv.at[plane, line]
+        copy = pltpu.make_async_remote_copy(
+            src_ref=coarse.at[plane, line], dst_ref=coarse.at[plane, line], send_sem=csend.at[0], recv_sem=sems,
+            device_id=(s, g), device_id_type=MESH,
+        )
+        if plane == 1:
+            copy.wait_recv()
+        else:
+            @pl.when(exists(plane - 1, 0))
+            def _():
+                copy.wait_recv()
+
+    def terms(ns, plane):
+        x = jnp.concatenate([coarse[plane, pl.ds(order[n], 1)][0] for n in ns], axis=0)
+        size = len(ns) * quarter
+        wide = dot(stacked(x), coarse_b[plane])
+        span = 9 * outs
+        wide = wide[:size, :span] + wide[:size, span:] + wide[size:, :span]
+        for k, n in enumerate(ns):
+            for b in range(3):
+                spot = pl.ds(pl.multiple_of((order[n] + 2 - b) * quarter, quarter), quarter)
+                sums[spot] = sums[spot] + wide[k * quarter : (k + 1) * quarter, b * 3 * outs : (b + 1) * 3 * outs]
+
+    def own(ns):
+        for n in ns:
+            if n:
+                landed(n, 1)
+                sideways(n)
+        terms(ns, 1)
+
+    def others(ns):
+        for plane in (0, 2):
+            for n in ns:
+                landed(n, plane)
+        for plane in (0, 2):
+            terms(ns, plane)
+
+    for plane in (0, 2):
+        @pl.when(jnp.logical_not(exists(plane - 1, 0)))
+        def _():
+            coarse[plane] = jnp.zeros(coarse.shape[1:], F32)
+
+    sums[...] = jnp.zeros(sums.shape, F32)
+    stages = [[0]] + [list(range(n, min(n + 2, groups))) for n in range(1, groups, 2)]
+    for k, stage in enumerate(stages):
+        own(stage)
+        if 0 < k < len(stages) - 1:
+            others(stages[k - 1])
+    for stage in stages[-2:]:
+        others(stage)
+    x = sums[quarter : quarter + cells]
+    before, _ = beside(x[:, :outs], quarter)
+    _, after = beside(x[:, 2 * outs :], quarter)
+    out[...] = gelu(before + x[:, outs : 2 * outs] + after).T
 
     arrive(first, False)
     arrive(again, False)
-    for copy in spread + sum(crossed + forward, []) + sent:
+    for copy in spread + sum(crossed + forward, []):
         copy.wait_send()
-
-    @pl.when(exists(1, 0))
-    def _():
-        up.wait_send()
-
-    @pl.when(exists(-1, 0))
-    def _():
-        down.wait_send()
+    for there, copy in sent:
+        @pl.when(there)
+        def _():
+            copy.wait_send()
 
 
 def per_device(slabs, groups, volume, conv_fine, down_first, conv_middle, down_second, conv_coarse):
@@ -461,27 +500,23 @@
             V(down1.shape, F32),
             V((8 * c1, 2 * c2), BF16),
             V(middle.shape, F32),
-            V((3, 12 * c2, 2 * c2), BF16),
-            V((3, 12 * c2, 2 * c2), BF16),
+            V((3 * h2 * c2, 3 * h2 * c2), BF16),
+            V((3 * h2 * c2, 3 * h2 * c2), BF16),
+            V((2, 3 * c2, 3 * c2), BF16),
+            V((2, 3 * c2, 3 * c2), BF16),
             V((d2 + 2, h2 + 2, half, c2), F32),
-            V((2, d2 + 2, half, 12 * c2), BF16),
+            V((d2 + 2, half, (h2 + 2) * c2), BF16),
+            V((d2 + 2, half, (h2 + 2) * c2), BF16),
             V((h2, d2 * half, c2), F32),
             V((groups,) + shard.shape, F32),
             V(coarse_w.shape, F32),
-            V((3, 3 * c3, 2 * c4), BF16),
-            V((3, 3 * c3, 2 * c4), BF16),
-            V((3, 3 * c3, c4), BF16),
-            V((3, 3 * c3, c4), BF16),
-            V((groups, quarter, c3), F32),
-            V((2, cells + 2 * quarter, 3 * c3), BF16),
-            V((cells, c4), F32),
-            V((cells, c4), F32),
-            V((cells, c4), F32),
-            V((cells, c4), F32),
+            V((3, c3, 18 * c4), BF16),
+            V((3, groups, quarter, c3), F32),
+            V((cells + 2 * quarter, 3 * c4), F32),
             dma((6,)),
             dma((8,)), dma((8,)), dma((8,)), dma((8,)),
-            dma((groups,)), dma((groups,)), dma((groups, 3)), dma((groups, 3)), dma((groups, 1)), dma((groups, 1)), dma((groups,)), dma((groups,)),
-            dma((2,)), dma((2,)),
+            dma((groups,)), dma((groups,)), dma((groups, 3)), dma((groups, 3)), dma((groups, 1)), dma((groups, 1)), dma((2 * groups,)), dma((groups,)),
+            dma((2, groups)), dma((3, groups)),
         ],
         compiler_params=pltpu.CompilerParams(
             collective_id=0, has_side_effects=True, vmem_limit_bytes=60 * 1024 * 1024

time: 33.2 us -> 32.7 us (0.985)
  Pallas kernels: 32.5 us -> 31.9 us
    pallas_call x1, Pallas kernels: 32.5 us -> 31.9 us  [per_device(): pl.pallas_call(functools.partial(kernel, slabs, groups), out_shape=pltpu....]
where the time goes in v3:
time: 32.7 us; the launch traced here: 32.6 us
  Pallas kernels  31.9 us (98%)
  local copies, waits for them, and re-layouts  0.63 us (2%)
    pallas_call x1, Pallas kernels, per_device(): pl.pallas_call(functools.partial(kernel, slabs, groups), out_shape=pltpu....  31.9 us

profile of v3, /device:TPU:1, one launch (start us, length us, event | category | flops | bytes accessed | tf_op | source)
XLA Modules:
  0.0 32.6 jit_solution(10128168503018821083)
XLA Ops:
  0.0 31.9 %shard_map.64 = f32[128,128]{1,0:T(8,128)S(1)} custom-call(f32[1024,128]{1,0:T(8,128)} %bitcast.15, f32[27,64,64]{2,1,0:T(8,128)} %bitcast.14, f32[2,256,128]{2,1,0:T(8,128)} %bitcast.16, f32[9,384,128]{2,1,0:T(8,128)} %bitcast.13, f32[8,64,128]{2,1,0:T(8,128)} %bitcast.17, f32[9,768,128]{2,1,0:T(8,128)} %bitcast.12), custom_call_target="tpu_custom_call" | custom-call | tf_op jit(solution)/shard_map/pallas_call | solution.py:485
  31.9 0.6 %copy.9 = f32[128,1,128]{2,1,0:T(1,128)} copy(f32[128,1,128]{2,1,0:T(1,128)S(1)} %bitcast.11) | data formatting | bytes 131072

commit v4 on v3

--- a/solution.py
+++ b/solution.py
@@ -57,7 +57,7 @@
     vol, fine, field, field_h, field_l, inner, outer, partial, turned, down1, down1_w, middle,
     mid_h, mid_l, side_h, side_l, second, second_h, second_l, level2, gathered, coarse_w, coarse_b,
     coarse, sums,
-    load_sem, send1, recv1, send2, recv2, wsend, wrecv, xsend, xrecv, fsend, frecv, csend, crecv, nsend, nrecv,
+    load_sem, ready, send1, recv1, send2, recv2, wsend, wrecv, xsend, xrecv, fsend, frecv, csend, crecv, nsend, nrecv,
 ):
     s, g = lax.axis_index("slab"), lax.axis_index("grp")
     depth, height, chans, width = (field.shape[0] - 2, field.shape[1] - 2) + field.shape[2:]
@@ -79,22 +79,13 @@
 
     barrier = pltpu.get_barrier_semaphore()
     heard = jnp.int32(0)
-    for ds, dg in WAYS:
+    for ds, dg in WAYS[:4]:
         there = exists(ds, dg)
         heard = heard + there.astype(jnp.int32)
 
         @pl.when(there)
         def _():
             pl.semaphore_signal(barrier, inc=1, device_id=(s + ds, g + dg), device_id_type=MESH)
-
-    for dg in range(2, groups):
-        for sign in (1, -1):
-            there = exists(0, sign * dg)
-            heard = heard + there.astype(jnp.int32)
-
-            @pl.when(there)
-            def _():
-                pl.semaphore_signal(barrier, inc=1, device_id=(s, g + sign * dg), device_id_type=MESH)
 
     sibling = s + 1 - 2 * lax.rem(s, 2)
     low, high = lax.rem(s // 2, 2), lax.rem(s // 4, 2)
@@ -107,18 +98,44 @@
     parity = lax.rem(s, 2)
     eighth = pl.ds((parity * 4 + lax.rem(s // 2, 4)) * (taps_of // 8), taps_of // 8)
     half_taps = pl.ds(parity * (taps_of // 2), taps_of // 2)
+    def nth(n):
+        spare = jnp.minimum(g, groups - 1 - g)
+        near = (n + 1) // 2 if n % 2 else -(n // 2)
+        away = jnp.where(2 * g < groups - 1, 1, -1)
+        return g + jnp.where(n <= 2 * spare, near, away * (n - spare))
+
+    order = [nth(n) for n in range(groups)]
     spread, crossed, forward = [], [], []
-    for j in range(1, groups):
+    rounds = max(1, groups - 2)
+
+    def spread_to(dg):
         copy = pltpu.make_async_remote_copy(
-            src_ref=shard.at[eighth],
-            dst_ref=gathered.at[g, eighth],
-            send_sem=wsend.at[j],
-            recv_sem=wrecv.at[j],
-            device_id=(s, lax.rem(g + j, groups)),
-            device_id_type=MESH,
+            src_ref=shard.at[eighth], dst_ref=gathered.at[g, eighth],
+            send_sem=wsend.at[dg + groups - 1], recv_sem=wrecv.at[g],
+            device_id=(s, g + dg), device_id_type=MESH,
         )
-        copy.start()
-        spread.append(copy)
+
+        @pl.when(exists(0, dg))
+        def _():
+            copy.start()
+
+        spread.append((exists(0, dg), copy))
+
+    def announce(n):
+        for ds, dg in WAYS[:4] if n == 0 else WAYS[2:4]:
+            @pl.when(exists(ds, dg))
+            def _():
+                pl.semaphore_signal(ready.at[n], inc=1, device_id=(s + ds, g + dg), device_id_type=MESH)
+
+    def listen(n):
+        count = jnp.int32(0)
+        for ds, dg in WAYS[:4] if n == 0 else WAYS[2:4]:
+            count = count + exists(ds, dg).astype(jnp.int32)
+        pl.semaphore_wait(ready.at[n], count)
+
+    announce(0)
+    for dg in (1, -1):
+        spread_to(dg)
 
     loads[0].wait()
     lines = depth * height
@@ -134,10 +151,12 @@
             return pl.ds(1, size)
         return pl.ds(0 if way > 0 else size + 1, 1)
 
-    def halo(src, offset, buf, sends, recvs):
+    def halo(src, offset, buf, sends, recvs, between=None):
         nd, nh = buf.shape[0] - 2, buf.shape[1] - 2
         copies = []
         for k, (ds, dg) in enumerate(WAYS):
+            if k == 4 and between is not None:
+                between()
             copies.append(
                 pltpu.make_async_remote_copy(
                     src_ref=src.at[part(ds, nd, offset), part(dg, nh, offset)],
@@ -173,26 +192,43 @@
                 def _():
                     copies[k].wait_send()
 
-    first = halo(field, 1, field, send1, recv1)
+    def further():
+        for n in range(rounds):
+            listen(n)
+            if n + 1 < rounds:
+                announce(n + 1)
+            if n + 2 < groups:
+                for dg in (n + 2, -n - 2):
+                    spread_to(dg)
+
+    first = halo(field, 1, field, send1, recv1, further)
 
     def hand_on(arrived, out_copies, piece, sends, recvs, peers):
-        for j in range(1, groups):
-            for copy in arrived[j - 1]:
+        for n in range(1, groups):
+            source = order[n]
+            for copy in arrived(n, source):
                 copy.wait_recv()
-            source = lax.rem(g + groups - j, groups)
             made = []
             for k, peer in enumerate(peers):
                 copy = pltpu.make_async_remote_copy(
                     src_ref=gathered.at[source, piece],
                     dst_ref=gathered.at[source, piece],
-                    send_sem=sends.at[j, k],
-                    recv_sem=recvs.at[j, k],
+                    send_sem=sends.at[n, k],
+                    recv_sem=recvs.at[n, k],
                     device_id=(peer, g),
                     device_id_type=MESH,
                 )
                 copy.start()
                 made.append(copy)
             out_copies.append(made)
+
+    def from_group(n, source):
+        return [
+            pltpu.make_async_remote_copy(
+                src_ref=gathered.at[source, eighth], dst_ref=gathered.at[source, eighth],
+                send_sem=wsend.at[0], recv_sem=wrecv.at[source], device_id=(s, g), device_id_type=MESH,
+            )
+        ]
 
     loads[1].wait()
     blocks = height // 2
@@ -289,7 +325,7 @@
             narrow(pl.ds(jnp.where(k == 0, 0, depth + 1), 1), slice(1, height + 1))
         for block in range(blocks):
             partial[block, k] = dot(inner[block], across(2 * block + within[block][0], len(within[block]), 2 * k))
-    hand_on([[c] for c in spread], crossed, eighth, xsend, xrecv, crossings)
+    hand_on(from_group, crossed, eighth, xsend, xrecv, crossings)
     arrive(first, True, range(2, len(WAYS)))
     for h in (0, height + 1):
         narrow(slice(0, depth + 2), slice(h, h + 1))
@@ -335,7 +371,7 @@
     for h in range(1, h2 + 1):
         thin(h)
     total = product(gathered_taps(c2, (1 + h2) * c2), (mid_h[...], mid_l[...]))
-    hand_on(crossed, forward, half_taps, fsend, frecv, [sibling])
+    hand_on(lambda n, source: crossed[n - 1], forward, half_taps, fsend, frecv, [sibling])
     arrive(again, True, range(2, len(WAYS)))
     for h in (0, h2 + 1):
         thin(h)
@@ -369,12 +405,6 @@
     coarse[1, pl.ds(g, 1)] = share[None]
     cells = groups * quarter
 
-    def nth(n):
-        spare = jnp.minimum(g, groups - 1 - g)
-        near = (n + 1) // 2 if n % 2 else -(n // 2)
-        away = jnp.where(2 * g < groups - 1, 1, -1)
-        return g + jnp.where(n <= 2 * spare, near, away * (n - spare))
-
     sent = []
 
     def send(there, line, plane, peer, sends, recvs):
@@ -389,8 +419,6 @@
 
         sent.append((there, copy))
 
-    order = [nth(n) for n in range(groups)]
-
     def sideways(n):
         for k, ds in enumerate((1, -1)):
             send(exists(ds, 0), order[n], 1 - ds, (s + ds, g), nsend.at[k, n], nrecv.at[1 - ds, order[n]])
@@ -401,12 +429,13 @@
 
     def landed(n, plane):
         line = order[n]
-        sems = crecv.at[line] if plane == 1 else nrecv.at[plane, line]
+        mine = isinstance(plane, int) and plane == 1
+        sems = crecv.at[line] if mine else nrecv.at[plane, line]
         copy = pltpu.make_async_remote_copy(
             src_ref=coarse.at[plane, line], dst_ref=coarse.at[plane, line], send_sem=csend.at[0], recv_sem=sems,
             device_id=(s, g), device_id_type=MESH,
         )
-        if plane == 1:
+        if mine:
             copy.wait_recv()
         else:
             @pl.when(exists(plane - 1, 0))
@@ -432,10 +461,9 @@
         terms(ns, 1)
 
     def others(ns):
-        for plane in (0, 2):
+        for plane in (2 - 2 * parity, 2 * parity):
             for n in ns:
                 landed(n, plane)
-        for plane in (0, 2):
             terms(ns, plane)
 
     for plane in (0, 2):
@@ -458,9 +486,9 @@
 
     arrive(first, False)
     arrive(again, False)
-    for copy in spread + sum(crossed + forward, []):
+    for copy in sum(crossed + forward, []):
         copy.wait_send()
-    for there, copy in sent:
+    for there, copy in spread + sent:
         @pl.when(there)
         def _():
             copy.wait_send()
@@ -514,8 +542,9 @@
             V((3, groups, quarter, c3), F32),
             V((cells + 2 * quarter, 3 * c4), F32),
             dma((6,)),
+            pltpu.SemaphoreType.REGULAR((max(1, groups - 2),)),
             dma((8,)), dma((8,)), dma((8,)), dma((8,)),
-            dma((groups,)), dma((groups,)), dma((groups, 3)), dma((groups, 3)), dma((groups, 1)), dma((groups, 1)), dma((2 * groups,)), dma((groups,)),
+            dma((2 * groups,)), dma((groups,)), dma((groups, 3)), dma((groups, 3)), dma((groups, 1)), dma((groups, 1)), dma((2 * groups,)), dma((groups,)),
             dma((2, groups)), dma((3, groups)),
         ],
         compiler_params=pltpu.CompilerParams(

time: 32.7 us -> 32.4 us (level)
  no operation moved by 1% of the time
where the time goes in v4:
time: 32.4 us; the launch traced here: 32.3 us
  Pallas kernels  31.6 us (98%)
  local copies, waits for them, and re-layouts  0.63 us (2%)
    pallas_call x1, Pallas kernels, per_device(): pl.pallas_call(functools.partial(kernel, slabs, groups), out_shape=pltpu....  31.6 us

profile of v4, /device:TPU:1, one launch (start us, length us, event | category | flops | bytes accessed | tf_op | source)
XLA Modules:
  0.0 32.3 jit_solution(9086898471775954080)
XLA Ops:
  0.0 31.6 %shard_map.64 = f32[128,128]{1,0:T(8,128)S(1)} custom-call(f32[1024,128]{1,0:T(8,128)} %bitcast.15, f32[27,64,64]{2,1,0:T(8,128)} %bitcast.14, f32[2,256,128]{2,1,0:T(8,128)} %bitcast.16, f32[9,384,128]{2,1,0:T(8,128)} %bitcast.13, f32[8,64,128]{2,1,0:T(8,128)} %bitcast.17, f32[9,768,128]{2,1,0:T(8,128)} %bitcast.12), custom_call_target="tpu_custom_call" | custom-call | tf_op jit(solution)/shard_map/pallas_call | solution.py:513
  31.7 0.6 %copy.9 = f32[128,1,128]{2,1,0:T(1,128)} copy(f32[128,1,128]{2,1,0:T(1,128)S(1)} %bitcast.11) | data formatting | bytes 131072

commit v5 on v4

--- a/solution.py
+++ b/solution.py
@@ -57,7 +57,7 @@
     vol, fine, field, field_h, field_l, inner, outer, partial, turned, down1, down1_w, middle,
     mid_h, mid_l, side_h, side_l, second, second_h, second_l, level2, gathered, coarse_w, coarse_b,
     coarse, sums,
-    load_sem, ready, send1, recv1, send2, recv2, wsend, wrecv, xsend, xrecv, fsend, frecv, csend, crecv, nsend, nrecv,
+    load_sem, ready, face_sem, recv1, recv2, spread_sem, wrecv, xrecv, frecv, crecv, nrecv,
 ):
     s, g = lax.axis_index("slab"), lax.axis_index("grp")
     depth, height, chans, width = (field.shape[0] - 2, field.shape[1] - 2) + field.shape[2:]
@@ -105,21 +105,19 @@
         return g + jnp.where(n <= 2 * spare, near, away * (n - spare))
 
     order = [nth(n) for n in range(groups)]
-    spread, crossed, forward = [], [], []
     rounds = max(1, groups - 2)
 
-    def spread_to(dg):
-        copy = pltpu.make_async_remote_copy(
+    def settle(sem, view):
+        pltpu.make_async_remote_copy(
+            src_ref=view, dst_ref=view, send_sem=sem, recv_sem=sem, device_id=(s, g), device_id_type=MESH
+        ).wait_recv()
+
+    def spread_to(n):
+        pltpu.make_async_remote_copy(
             src_ref=shard.at[eighth], dst_ref=gathered.at[g, eighth],
-            send_sem=wsend.at[dg + groups - 1], recv_sem=wrecv.at[g],
-            device_id=(s, g + dg), device_id_type=MESH,
-        )
-
-        @pl.when(exists(0, dg))
-        def _():
-            copy.start()
-
-        spread.append((exists(0, dg), copy))
+            send_sem=spread_sem.at[0], recv_sem=wrecv.at[lax.rem(g - order[n] - 1 + groups, groups)],
+            device_id=(s, order[n]), device_id_type=MESH,
+        ).start()
 
     def announce(n):
         for ds, dg in WAYS[:4] if n == 0 else WAYS[2:4]:
@@ -134,8 +132,7 @@
         pl.semaphore_wait(ready.at[n], count)
 
     announce(0)
-    for dg in (1, -1):
-        spread_to(dg)
+    spread_to(1)
 
     loads[0].wait()
     lines = depth * height
@@ -198,37 +195,22 @@
             if n + 1 < rounds:
                 announce(n + 1)
             if n + 2 < groups:
-                for dg in (n + 2, -n - 2):
-                    spread_to(dg)
-
-    first = halo(field, 1, field, send1, recv1, further)
-
-    def hand_on(arrived, out_copies, piece, sends, recvs, peers):
+                spread_to(n + 2)
+
+    first = halo(field, 1, field, face_sem, recv1, further)
+
+    foreign = slice(0, groups - 1)
+
+    def hand_on(piece, sends, recvs, peers, spread=False):
         for n in range(1, groups):
             source = order[n]
-            for copy in arrived(n, source):
-                copy.wait_recv()
-            made = []
-            for k, peer in enumerate(peers):
-                copy = pltpu.make_async_remote_copy(
-                    src_ref=gathered.at[source, piece],
-                    dst_ref=gathered.at[source, piece],
-                    send_sem=sends.at[n, k],
-                    recv_sem=recvs.at[n, k],
-                    device_id=(peer, g),
-                    device_id_type=MESH,
-                )
-                copy.start()
-                made.append(copy)
-            out_copies.append(made)
-
-    def from_group(n, source):
-        return [
-            pltpu.make_async_remote_copy(
-                src_ref=gathered.at[source, eighth], dst_ref=gathered.at[source, eighth],
-                send_sem=wsend.at[0], recv_sem=wrecv.at[source], device_id=(s, g), device_id_type=MESH,
-            )
-        ]
+            if spread:
+                settle(wrecv.at[lax.rem(source - g - 1 + groups, groups)], gathered.at[source, eighth])
+            for peer in peers:
+                pltpu.make_async_remote_copy(
+                    src_ref=gathered.at[source, piece], dst_ref=gathered.at[source, piece],
+                    send_sem=sends, recv_sem=recvs, device_id=(peer, g), device_id_type=MESH,
+                ).start()
 
     loads[1].wait()
     blocks = height // 2
@@ -325,7 +307,7 @@
             narrow(pl.ds(jnp.where(k == 0, 0, depth + 1), 1), slice(1, height + 1))
         for block in range(blocks):
             partial[block, k] = dot(inner[block], across(2 * block + within[block][0], len(within[block]), 2 * k))
-    hand_on(from_group, crossed, eighth, xsend, xrecv, crossings)
+    hand_on(eighth, load_sem.at[0], xrecv.at[0], crossings, True)
     arrive(first, True, range(2, len(WAYS)))
     for h in (0, height + 1):
         narrow(slice(0, depth + 2), slice(h, h + 1))
@@ -353,7 +335,8 @@
     total = total.reshape(h2, d2, half, c2)
     for h in range(h2):
         second[1 : d2 + 1, 1 + h] = total[h]
-    again = halo(second, 1, second, send2, recv2)
+    arrive(first, False)
+    again = halo(second, 1, second, face_sem, recv2)
     prepare_coarse()
     def thin(h):
         spot = slice(h * c2, (h + 1) * c2)
@@ -371,7 +354,8 @@
     for h in range(1, h2 + 1):
         thin(h)
     total = product(gathered_taps(c2, (1 + h2) * c2), (mid_h[...], mid_l[...]))
-    hand_on(lambda n, source: crossed[n - 1], forward, half_taps, fsend, frecv, [sibling])
+    settle(xrecv.at[0], gathered.at[foreign, 0 : 3 * (taps_of // 8)])
+    hand_on(half_taps, load_sem.at[1], frecv.at[0], [sibling])
     arrive(again, True, range(2, len(WAYS)))
     for h in (0, h2 + 1):
         thin(h)
@@ -396,51 +380,33 @@
         axis=1,
     )
     lhs = stacked(lhs)
-    for made in forward:
-        made[0].wait_recv()
-    weights = jnp.concatenate(
+    settle(frecv.at[0], gathered.at[foreign, 0 : taps_of // 2])
+    filters = jnp.concatenate(
         [gathered[:, t].reshape(groups * shard.shape[1], c2) for t in range(taps_of)], axis=1
     )
-    share = product(lhs, split(weights), (((1,), (1,)), ((), ())))
+    share = product(lhs, split(filters), (((1,), (1,)), ((), ())))
     coarse[1, pl.ds(g, 1)] = share[None]
     cells = groups * quarter
 
-    sent = []
-
-    def send(there, line, plane, peer, sends, recvs):
-        copy = pltpu.make_async_remote_copy(
-            src_ref=coarse.at[1, line], dst_ref=coarse.at[plane, line], send_sem=sends, recv_sem=recvs,
-            device_id=peer, device_id_type=MESH,
-        )
-
-        @pl.when(there)
-        def _():
-            copy.start()
-
-        sent.append((there, copy))
-
     def sideways(n):
         for k, ds in enumerate((1, -1)):
-            send(exists(ds, 0), order[n], 1 - ds, (s + ds, g), nsend.at[k, n], nrecv.at[1 - ds, order[n]])
-
-    for k, dg in enumerate(d for d in range(1 - groups, groups) if d):
-        send(exists(0, dg), g, 1, (s, g + dg), csend.at[k], crecv.at[g])
+            copy = pltpu.make_async_remote_copy(
+                src_ref=coarse.at[1, order[n]], dst_ref=coarse.at[1 - ds, order[n]],
+                send_sem=load_sem.at[3 + k], recv_sem=nrecv.at[k, (n + 1) // 2],
+                device_id=(s + ds, g), device_id_type=MESH,
+            )
+
+            @pl.when(exists(ds, 0))
+            def _():
+                copy.start()
+
+    for n in range(groups - 1, 0, -1):
+        pltpu.make_async_remote_copy(
+            src_ref=coarse.at[1, g], dst_ref=coarse.at[1, g],
+            send_sem=load_sem.at[2], recv_sem=crecv.at[lax.rem(g - order[n] - 1 + groups, groups)],
+            device_id=(s, order[n]), device_id_type=MESH,
+        ).start()
     sideways(0)
-
-    def landed(n, plane):
-        line = order[n]
-        mine = isinstance(plane, int) and plane == 1
-        sems = crecv.at[line] if mine else nrecv.at[plane, line]
-        copy = pltpu.make_async_remote_copy(
-            src_ref=coarse.at[plane, line], dst_ref=coarse.at[plane, line], send_sem=csend.at[0], recv_sem=sems,
-            device_id=(s, g), device_id_type=MESH,
-        )
-        if mine:
-            copy.wait_recv()
-        else:
-            @pl.when(exists(plane - 1, 0))
-            def _():
-                copy.wait_recv()
 
     def terms(ns, plane):
         x = jnp.concatenate([coarse[plane, pl.ds(order[n], 1)][0] for n in ns], axis=0)
@@ -456,14 +422,17 @@
     def own(ns):
         for n in ns:
             if n:
-                landed(n, 1)
+                settle(crecv.at[lax.rem(order[n] - g - 1 + groups, groups)], coarse.at[1, order[n]])
                 sideways(n)
         terms(ns, 1)
 
     def others(ns):
         for plane in (2 - 2 * parity, 2 * parity):
-            for n in ns:
-                landed(n, plane)
+
+            @pl.when(exists(plane - 1, 0))
+            def _():
+                settle(nrecv.at[plane // 2, (ns[0] + 1) // 2], coarse.at[1, 0 : len(ns)])
+
             terms(ns, plane)
 
     for plane in (0, 2):
@@ -484,14 +453,15 @@
     _, after = beside(x[:, 2 * outs :], quarter)
     out[...] = gelu(before + x[:, outs : 2 * outs] + after).T
 
-    arrive(first, False)
     arrive(again, False)
-    for copy in sum(crossed + forward, []):
-        copy.wait_send()
-    for there, copy in spread + sent:
-        @pl.when(there)
+    settle(spread_sem.at[0], gathered.at[foreign, 0 : taps_of // 8])
+    settle(load_sem.at[0], gathered.at[foreign, 0 : 3 * (taps_of // 8)])
+    settle(load_sem.at[1], gathered.at[foreign, 0 : taps_of // 2])
+    settle(load_sem.at[2], coarse.at[1, 0 : groups - 1])
+    for k, ds in enumerate((1, -1)):
+        @pl.when(exists(ds, 0))
         def _():
-            copy.wait_send()
+            settle(load_sem.at[3 + k], coarse.at[1])
 
 
 def per_device(slabs, groups, volume, conv_fine, down_first, conv_middle, down_second, conv_coarse):
@@ -543,9 +513,8 @@
             V((cells + 2 * quarter, 3 * c4), F32),
             dma((6,)),
             pltpu.SemaphoreType.REGULAR((max(1, groups - 2),)),
-            dma((8,)), dma((8,)), dma((8,)), dma((8,)),
-            dma((2 * groups,)), dma((groups,)), dma((groups, 3)), dma((groups, 3)), dma((groups, 1)), dma((groups, 1)), dma((2 * groups,)), dma((groups,)),
-            dma((2, groups)), dma((3, groups)),
+            dma((8,)), dma((8,)), dma((8,)),
+            dma((1,)), dma((groups - 1,)), dma((1,)), dma((1,)), dma((groups - 1,)), dma((2, 1 + groups // 2)),
         ],
         compiler_params=pltpu.CompilerParams(
             collective_id=0, has_side_effects=True, vmem_limit_bytes=60 * 1024 * 1024

time: 32.4 us -> 31.7 us (0.978)
  Pallas kernels: 31.6 us -> 31 us
    pallas_call x1, Pallas kernels: 31.6 us -> 31 us  [per_device(): pl.pallas_call(functools.partial(kernel, slabs, groups), out_shape=pltpu....]
where the time goes in v5:
time: 31.7 us; the launch traced here: 31.6 us
  Pallas kernels  31 us (98%)
  local copies, waits for them, and re-layouts  0.63 us (2%)
    pallas_call x1, Pallas kernels, per_device(): pl.pallas_call(functools.partial(kernel, slabs, groups), out_shape=pltpu....  31 us

profile of v5, /device:TPU:1, one launch (start us, length us, event | category | flops | bytes accessed | tf_op | source)
XLA Modules:
  0.0 31.6 jit_solution(17706557326674561132)
XLA Ops:
  0.0 31.0 %shard_map.64 = f32[128,128]{1,0:T(8,128)S(1)} custom-call(f32[1024,128]{1,0:T(8,128)} %bitcast.15, f32[27,64,64]{2,1,0:T(8,128)} %bitcast.14, f32[2,256,128]{2,1,0:T(8,128)} %bitcast.16, f32[9,384,128]{2,1,0:T(8,128)} %bitcast.13, f32[8,64,128]{2,1,0:T(8,128)} %bitcast.17, f32[9,768,128]{2,1,0:T(8,128)} %bitcast.12), custom_call_target="tpu_custom_call" | custom-call | tf_op jit(solution)/shard_map/pallas_call | solution.py:483
  31.0 0.6 %copy.9 = f32[128,1,128]{2,1,0:T(1,128)} copy(f32[128,1,128]{2,1,0:T(1,128)S(1)} %bitcast.11) | data formatting | bytes 131072

commit v6 on v5

--- a/solution.py
+++ b/solution.py
@@ -112,12 +112,16 @@
             src_ref=view, dst_ref=view, send_sem=sem, recv_sem=sem, device_id=(s, g), device_id_type=MESH
         ).wait_recv()
 
-    def spread_to(n):
-        pltpu.make_async_remote_copy(
+    def spread_to(n, there=True):
+        copy = pltpu.make_async_remote_copy(
             src_ref=shard.at[eighth], dst_ref=gathered.at[g, eighth],
             send_sem=spread_sem.at[0], recv_sem=wrecv.at[lax.rem(g - order[n] - 1 + groups, groups)],
             device_id=(s, order[n]), device_id_type=MESH,
-        ).start()
+        )
+
+        @pl.when(there)
+        def _():
+            copy.start()
 
     def announce(n):
         for ds, dg in WAYS[:4] if n == 0 else WAYS[2:4]:
@@ -133,6 +137,9 @@
 
     announce(0)
     spread_to(1)
+    inside = (g > 0) & (g < groups - 1)
+    if groups > 2:
+        spread_to(2, inside)
 
     loads[0].wait()
     lines = depth * height
@@ -189,20 +196,19 @@
                 def _():
                     copies[k].wait_send()
 
-    def further():
-        for n in range(rounds):
-            listen(n)
-            if n + 1 < rounds:
-                announce(n + 1)
-            if n + 2 < groups:
-                spread_to(n + 2)
-
-    first = halo(field, 1, field, face_sem, recv1, further)
+    def vouch(n):
+        listen(n)
+        if n + 1 < rounds:
+            announce(n + 1)
+        if n + 2 < groups:
+            spread_to(n + 2, jnp.logical_not(inside) if n == 0 else True)
+
+    first = halo(field, 1, field, face_sem, recv1, lambda: vouch(0))
 
     foreign = slice(0, groups - 1)
 
-    def hand_on(piece, sends, recvs, peers, spread=False):
-        for n in range(1, groups):
+    def hand_on(piece, sends, recvs, peers, spread=False, ns=range(1, groups)):
+        for n in ns:
             source = order[n]
             if spread:
                 settle(wrecv.at[lax.rem(source - g - 1 + groups, groups)], gathered.at[source, eighth])
@@ -239,6 +245,8 @@
     for k, (_, _, b) in enumerate(beyond):
         parts = [jnp.concatenate(taps_at(x, b), axis=1) for x in both]
         outer[k] = jnp.concatenate([parts[0], parts[1], parts[0]], axis=1)
+    for n in range(1, rounds):
+        vouch(n)
     d2, h2, c2 = depth // 2, blocks, down1.shape[2]
     for load in loads[2:5]:
         load.wait()
@@ -297,6 +305,8 @@
     pairs = [jnp.where(parity == 0, d2 - 1, 0)] + list(range(1, d2 - 1))
     pairs.append(d2 - 1 - pairs[0])
     for n, k in enumerate(pairs):
+        if n == d2 - 1:
+            hand_on(eighth, load_sem.at[0], xrecv.at[0], crossings, True, (1,))
         if n in (0, d2 - 1):
             for way in range(2):
                 mine = (parity == 1 - way) if n == 0 else (parity == way)
@@ -307,7 +317,7 @@
             narrow(pl.ds(jnp.where(k == 0, 0, depth + 1), 1), slice(1, height + 1))
         for block in range(blocks):
             partial[block, k] = dot(inner[block], across(2 * block + within[block][0], len(within[block]), 2 * k))
-    hand_on(eighth, load_sem.at[0], xrecv.at[0], crossings, True)
+    hand_on(eighth, load_sem.at[0], xrecv.at[0], crossings, True, range(2, groups))
     arrive(first, True, range(2, len(WAYS)))
     for h in (0, height + 1):
         narrow(slice(0, depth + 2), slice(h, h + 1))

time: 31.7 us -> 30.6 us (0.965)
  Pallas kernels: 31 us -> 29.8 us
    pallas_call x1, Pallas kernels: 31 us -> 29.8 us  [per_device(): pl.pallas_call(functools.partial(kernel, slabs, groups), out_shape=pltpu....]
where the time goes in v6:
time: 30.6 us; the launch traced here: 30.4 us
  Pallas kernels  29.8 us (97%)
  local copies, waits for them, and re-layouts  0.63 us (2%)
    pallas_call x1, Pallas kernels, per_device(): pl.pallas_call(functools.partial(kernel, slabs, groups), out_shape=pltpu....  29.8 us
    unnamed x1, local copies, waits for them, and re-layouts  0.63 us

profile of v6, /device:TPU:1, one launch (start us, length us, event | category | flops | bytes accessed | tf_op | source)
XLA Modules:
  0.0 30.4 jit_solution(5898416857552932134)
XLA Ops:
  0.0 29.8 %shard_map.64 = f32[128,128]{1,0:T(8,128)S(1)} custom-call(f32[1024,128]{1,0:T(8,128)} %bitcast.15, f32[27,64,64]{2,1,0:T(8,128)} %bitcast.14, f32[2,256,128]{2,1,0:T(8,128)} %bitcast.16, f32[9,384,128]{2,1,0:T(8,128)} %bitcast.13, f32[8,64,128]{2,1,0:T(8,128)} %bitcast.17, f32[9,768,128]{2,1,0:T(8,128)} %bitcast.12), custom_call_target="tpu_custom_call" | custom-call | tf_op jit(solution)/shard_map/pallas_call | solution.py:493
  29.8 0.6 %copy.9 = f32[128,1,128]{2,1,0:T(1,128)} copy(f32[128,1,128]{2,1,0:T(1,128)S(1)} %bitcast.11) | data formatting | bytes 131072

commit v7 on v6

--- a/solution.py
+++ b/solution.py
@@ -360,12 +360,12 @@
             )
         return jnp.concatenate(parts, axis=0)
 
+    settle(xrecv.at[0], gathered.at[foreign, 0 : 3 * (taps_of // 8)])
+    hand_on(half_taps, load_sem.at[1], frecv.at[0], [sibling])
     arrive(again, True, range(0, 2))
     for h in range(1, h2 + 1):
         thin(h)
     total = product(gathered_taps(c2, (1 + h2) * c2), (mid_h[...], mid_l[...]))
-    settle(xrecv.at[0], gathered.at[foreign, 0 : 3 * (taps_of // 8)])
-    hand_on(half_taps, load_sem.at[1], frecv.at[0], [sibling])
     arrive(again, True, range(2, len(WAYS)))
     for h in (0, h2 + 1):
         thin(h)
@@ -454,9 +454,9 @@
     stages = [[0]] + [list(range(n, min(n + 2, groups))) for n in range(1, groups, 2)]
     for k, stage in enumerate(stages):
         own(stage)
-        if 0 < k < len(stages) - 1:
+        if 0 < k < len(stages) - 2:
             others(stages[k - 1])
-    for stage in stages[-2:]:
+    for stage in stages[max(0, len(stages) - 3) :]:
         others(stage)
     x = sums[quarter : quarter + cells]
     before, _ = beside(x[:, :outs], quarter)

time: 30.6 us -> 29.7 us (0.971); the launches traced: 30.4 us -> 29.1 us
  Pallas kernels: 29.8 us -> 28.5 us
    pallas_call x1, Pallas kernels: 29.8 us -> 28.5 us  [per_device(): pl.pallas_call(functools.partial(kernel, slabs, groups), out_shape=pltpu....]
where the time goes in v7:
time: 29.7 us; the launch traced here: 29.1 us
  Pallas kernels  28.5 us (96%)
  local copies, waits for them, and re-layouts  0.63 us (2%)
    pallas_call x1, Pallas kernels, per_device(): pl.pallas_call(functools.partial(kernel, slabs, groups), out_shape=pltpu....  28.5 us
    unnamed x1, local copies, waits for them, and re-layouts  0.63 us

profile of v7, /device:TPU:1, one launch (start us, length us, event | category | flops | bytes accessed | tf_op | source)
XLA Modules:
  0.0 29.1 jit_solution(9473655040051381589)
XLA Ops:
  0.0 28.5 %shard_map.64 = f32[128,128]{1,0:T(8,128)S(1)} custom-call(f32[1024,128]{1,0:T(8,128)} %bitcast.15, f32[27,64,64]{2,1,0:T(8,128)} %bitcast.14, f32[2,256,128]{2,1,0:T(8,128)} %bitcast.16, f32[9,384,128]{2,1,0:T(8,128)} %bitcast.13, f32[8,64,128]{2,1,0:T(8,128)} %bitcast.17, f32[9,768,128]{2,1,0:T(8,128)} %bitcast.12), custom_call_target="tpu_custom_call" | custom-call | tf_op jit(solution)/shard_map/pallas_call | solution.py:493
  28.5 0.6 %copy.9 = f32[128,1,128]{2,1,0:T(1,128)} copy(f32[128,1,128]{2,1,0:T(1,128)S(1)} %bitcast.11) | data formatting | bytes 131072

commit v8 on v7

--- a/solution.py
+++ b/solution.py
@@ -452,10 +452,10 @@
 
     sums[...] = jnp.zeros(sums.shape, F32)
     stages = [[0]] + [list(range(n, min(n + 2, groups))) for n in range(1, groups, 2)]
-    for k, stage in enumerate(stages):
-        own(stage)
-        if 0 < k < len(stages) - 2:
-            others(stages[k - 1])
+    own(stages[0])
+    own(list(range(1, groups)))
+    for stage in stages[: max(0, len(stages) - 3)]:
+        others(stage)
     for stage in stages[max(0, len(stages) - 3) :]:
         others(stage)
     x = sums[quarter : quarter + cells]

time: 29.7 us -> 29.7 us (level)
  no operation moved by 1% of the time
where the time goes in v8:
time: 29.7 us; the launch traced here: 29.1 us
  Pallas kernels  28.5 us (96%)
  local copies, waits for them, and re-layouts  0.63 us (2%)
    pallas_call x1, Pallas kernels, per_device(): pl.pallas_call(functools.partial(kernel, slabs, groups), out_shape=pltpu....  28.5 us
    unnamed x1, local copies, waits for them, and re-layouts  0.63 us

profile of v8, /device:TPU:1, one launch (start us, length us, event | category | flops | bytes accessed | tf_op | source)
XLA Modules:
  0.0 29.1 jit_solution(11491830291086496069)
XLA Ops:
  0.0 28.5 %shard_map.64 = f32[128,128]{1,0:T(8,128)S(1)} custom-call(f32[1024,128]{1,0:T(8,128)} %bitcast.15, f32[27,64,64]{2,1,0:T(8,128)} %bitcast.14, f32[2,256,128]{2,1,0:T(8,128)} %bitcast.16, f32[9,384,128]{2,1,0:T(8,128)} %bitcast.13, f32[8,64,128]{2,1,0:T(8,128)} %bitcast.17, f32[9,768,128]{2,1,0:T(8,128)} %bitcast.12), custom_call_target="tpu_custom_call" | custom-call | tf_op jit(solution)/shard_map/pallas_call | solution.py:493
  28.5 0.6 %copy.9 = f32[128,1,128]{2,1,0:T(1,128)} copy(f32[128,1,128]{2,1,0:T(1,128)S(1)} %bitcast.11) | data formatting | bytes 131072
